TPU v7x, 512 devices: a whole 4x8x8 slice. The times are simulated.
512 devices in a mesh: rows: 64 (over y, x, core), cols: 8 (over z).
Axes of the slice: x: 4, y: 8, z: 8, core: 2. Of those that a mesh axis runs over, the one named last changes fastest.
Arguments:
- fact_cells: bfloat16 [3072, 32, 512], P('rows', 'cols'), may hold values from -6 to 6
- gain_col: float32 [512], replicated, may hold values from 0.1 to 1.9
- w_qkv: bfloat16 [512, 1536], replicated, may hold values from -0.25 to 0.25
- w_col_out: bfloat16 [512, 512], replicated, may hold values from -0.25 to 0.25
- gain_tile: float32 [512], replicated, may hold values from 0.1 to 1.9
- w_query: bfloat16 [512, 512], replicated, may hold values from -0.25 to 0.25
- w_tile_out: bfloat16 [512, 512], replicated, may hold values from -0.25 to 0.25
- tile_kv: bfloat16 [256, 128, 8, 128], P('rows', None, 'cols'), may hold values from -70 to 70
- tile_ids: int32 [64, 48], P('rows'), may hold values from -1 to 255, as said below
- key_mask: int32 [3072, 48], P('rows'), may hold values from 0 to 1, as said below
Outputs:
- layer_out: bfloat16 [3072, 32, 512], P('rows', 'cols')
Inputs may be any that keep to these rules, and one draw needn't show every extreme that they name: `tile_ids`: tile t is held by index t // 4 of rows. In every block the first slots, 36 of them or more, hold distinct tile ids and the rest hold -1; some block fills all 48 slots. The listed tiles of one block are held by distinct indices of rows. `key_mask`: 0 wherever the row's block holds -1 in that slot; 1 in slot 0 of every row.
All inputs are finite; a program needn't handle non-finite values.
Results may differ from a plain program's by a relative error of at most 0.023.
The roundings to bfloat16 on the way count: a program that leaves them out, or rounds other values in their place, can miss the bound.
Values may be sent and summed in bfloat16 or wider, within the bound.
A program may use at most 64 MiB of HBM per device.

v0:
```python
import jax
import jax.numpy as jnp
from jax import lax
from jax.sharding import PartitionSpec as P


def rms_scale(values, gain_vec):
    mean_sq = jnp.mean(values * values, axis=-1, keepdims=True)
    return values * lax.rsqrt(mean_sq + 1e-05) * gain_vec


def soft_weights(scores, axes):
    row_top = jnp.max(scores, axis=axes, keepdims=True)
    expo_vals = jnp.exp(scores - row_top)
    return (expo_vals / jnp.sum(expo_vals, axis=axes, keepdims=True)).astype(jnp.bfloat16)


def column_attend(queries, keyvals, head_size):
    key_part = keyvals[..., :head_size]
    val_part = keyvals[..., head_size:]
    scores = jnp.einsum(
        "rchd,rkhd->rhck", queries, key_part, preferred_element_type=jnp.float32
    ) * head_size ** (-0.5)
    col_weights = soft_weights(scores, (3,))
    return jnp.einsum(
        "rhck,rkhd->rchd", col_weights, val_part, preferred_element_type=jnp.float32
    ).astype(jnp.bfloat16)


def tile_attend(queries, fetched, key_mask, head_size):
    key_part = fetched[..., :head_size]
    val_part = fetched[..., head_size:]
    row_count, col_count, head_count = queries.shape[:3]
    q_blocks = queries.reshape(row_count // 4, 4, col_count, head_count, head_size)
    m_blocks = key_mask.reshape(row_count // 4, 4, key_mask.shape[1])

    def one_block(block_pair):
        block_q, block_m = block_pair
        scores = jnp.einsum(
            "rchd,tkhd->rchtk", block_q, key_part, preferred_element_type=jnp.float32
        ) * head_size ** (-0.5)
        live_keys = (block_m > 0)[:, None, None, :, None]
        scores = jnp.where(live_keys, scores, -1e30)
        tile_weights = soft_weights(scores, (3, 4))
        return jnp.einsum(
            "rchtk,tkhd->rchd", tile_weights, val_part, preferred_element_type=jnp.float32
        ).astype(jnp.bfloat16)

    answer = lax.map(one_block, (q_blocks, m_blocks))
    return answer.reshape(row_count, col_count, head_count, head_size)


def fetch_all(tile_kv, tile_ids):
    gathered = lax.all_gather(tile_kv, "rows", axis=0, tiled=True)
    return jnp.take(gathered, jnp.maximum(tile_ids[0], 0), axis=0)


def project(normed, weight):
    return jnp.dot(normed.reshape(-1, weight.shape[0]), weight, preferred_element_type=jnp.float32)


def shards(
    fact_cells,
    gain_col,
    w_qkv,
    w_col_out,
    gain_tile,
    w_query,
    w_tile_out,
    tile_kv,
    tile_ids,
    key_mask,
):
    model_width = fact_cells.shape[2]
    head_size = tile_kv.shape[3] // 2
    heads_all = model_width // head_size
    fetched = fetch_all(tile_kv, tile_ids)
    row_count, col_local = (fact_cells.shape[0], fact_cells.shape[1])
    residual = fact_cells.astype(jnp.float32)
    normed = rms_scale(residual, gain_col).astype(jnp.bfloat16)
    packed = (
        project(normed, w_qkv)
        .astype(jnp.bfloat16)
        .reshape(row_count, col_local, 3, heads_all, head_size)
    )
    queries = packed[:, :, 0]
    keyvals = jnp.concatenate([packed[:, :, 1], packed[:, :, 2]], axis=-1)
    queries_h, keyvals_h = (
        lax.all_to_all(queries, "cols", split_axis=2, concat_axis=1, tiled=True),
        lax.all_to_all(keyvals, "cols", split_axis=2, concat_axis=1, tiled=True),
    )
    mixed_col = column_attend(queries_h, keyvals_h, head_size)
    mixed_back = lax.all_to_all(mixed_col, "cols", split_axis=1, concat_axis=2, tiled=True)
    residual = residual + project(mixed_back, w_col_out).reshape(residual.shape)
    normed2 = rms_scale(residual, gain_tile).astype(jnp.bfloat16)
    asked_q = (
        project(normed2, w_query)
        .astype(jnp.bfloat16)
        .reshape(row_count, col_local, heads_all, head_size)
    )
    asked_h = lax.all_to_all(asked_q, "cols", split_axis=2, concat_axis=1, tiled=True)
    answer = tile_attend(asked_h, fetched, key_mask, head_size)
    answer_back = lax.all_to_all(answer, "cols", split_axis=1, concat_axis=2, tiled=True)
    final_out = residual + project(answer_back, w_tile_out).reshape(residual.shape)
    return final_out.astype(jnp.bfloat16)


def solution(mesh):
    placed = (
        P("rows", "cols", None),
        P(),
        P(),
        P(),
        P(),
        P(),
        P(),
        P("rows", None, "cols", None),
        P("rows", None),
        P("rows", None),
    )
    return jax.shard_map(
        shards, mesh=mesh, in_specs=placed, out_specs=P("rows", "cols", None), check_vma=False
    )
```

profile of v0, /device:TPU:8, one launch (start us, length us, event | category | flops | bytes accessed | tf_op | source)
XLA Modules:
  0.0 198.4 jit_solution(1383678545264350636)
XLA Ops:
  7.3 1.1 fusion.30
  8.3 1.1 fusion.32
  11.1 1.0 reshape.174
  12.1 10.3 %all-to-all-start.1 = ((bf16[8,2,6144]{2,1,0:T(2,128)(2,1)}), bf16[8,2,6144]{2,1,0:T(2,128)(2,1)S(1)}, u32[]{:S(2)}, u32[]{:S(2)}) async-start(bf16[8,2,6144]{2,1,0:T(2,128)(2,1)} %reshape.174), calls=%async_computation.1 | async-start | bytes 393216 | tf_op jit(solution)/shard_map/all_to_all | solution.py:89
  22.8 1.3 pad_maximum_fusion
  24.2 8.8 %all-to-all-done.1 = bf16[8,2,6144]{2,1,0:T(2,128)(2,1)S(1)} async-done(((bf16[8,2,6144]{2,1,0:T(2,128)(2,1)}), bf16[8,2,6144]{2,1,0:T(2,128)(2,1)S(1)}, u32[]{:S(2)}, u32[]{:S(2)}) %all-to-all-start.1) | async-done | bytes 196640 | tf_op jit(solution)/shard_map/all_to_all | solution.py:89
  32.9 3.5 %all-to-all-start = ((bf16[48,4,8,128]{3,1,0,2:T(4,128)(2,1)}), bf16[48,4,8,128]{3,1,0,2:T(4,128)(2,1)S(1)}, u32[]{:S(2)}, u32[]{:S(2)}) async-start(bf16[48,4,8,128]{3,1,0,2:T(4,128)(2,1)} %pad_maximum_fusion), calls=%async_computation | async-start | bytes 786432 | tf_op jit(solution)/shard_map/all_to_all | solution.py:90
  37.0 12.4 %all-to-all-done = bf16[48,4,8,128]{3,1,0,2:T(4,128)(2,1)S(1)} async-done(((bf16[48,4,8,128]{3,1,0,2:T(4,128)(2,1)}), bf16[48,4,8,128]{3,1,0,2:T(4,128)(2,1)S(1)}, u32[]{:S(2)}, u32[]{:S(2)}) %all-to-all-start) | async-done | bytes 393248 | tf_op jit(solution)/shard_map/all_to_all | solution.py:90
  49.5 1.3 fusion.38
  50.8 1.6 fusion.26
  52.9 12.2 %all_to_all.78 = bf16[8,2,6144]{2,1,0:T(2,128)(2,1)S(1)} all-to-all(bf16[8,2,6144]{2,1,0:T(2,128)(2,1)S(1)} %reshape.176), channel_id=1, replica_groups=mesh['rows'=64,'cols'=8] {'cols'}, dimensions={0} | all-to-all | bytes 393216 | tf_op jit(solution)/shard_map/all_to_all | solution.py:93
  66.7 1.3 convolution_convert_fusion.2
  68.4 1.0 reshape.178
  69.3 3.6 %all-to-all-start.3 = ((bf16[8,2,6144]{2,1,0:T(2,128)(2,1)}), bf16[8,2,6144]{2,1,0:T(2,128)(2,1)S(1)}, u32[]{:S(2)}, u32[]{:S(2)}) async-start(bf16[8,2,6144]{2,1,0:T(2,128)(2,1)} %reshape.178), calls=%async_computation.3 | async-start | bytes 393216 | tf_op jit(solution)/shard_map/all_to_all | solution.py:101
  73.0 9.4 %all-to-all-done.3 = bf16[8,2,6144]{2,1,0:T(2,128)(2,1)S(1)} async-done(((bf16[8,2,6144]{2,1,0:T(2,128)(2,1)}), bf16[8,2,6144]{2,1,0:T(2,128)(2,1)S(1)}, u32[]{:S(2)}, u32[]{:S(2)}) %all-to-all-start.3) | async-done | bytes 196640 | tf_op jit(solution)/shard_map/all_to_all | solution.py:101
  83.8 20.0 %all-gather.2.cloned.1.call-done = bf16[256,128,1,128]{3,1,2,0:T(8,128)(2,1)} async-done(((bf16[4,128,1,128]{3,1,2,0:T(8,128)(2,1)}), bf16[256,128,1,128]{3,1,2,0:T(8,128)(2,1)}) %all-gather.2.cloned.1.call-update) | async-done | bytes 8388624 | tf_op jit(solution)/shard_map/all_gather | solution.py:54
  103.8 4.2 %gather_fusion = bf16[48,128,128]{2,1,0:T(8,128)(2,1)S(1)} fusion(bf16[256,128,128]{2,1,0:T(8,128)(2,1)} %bitcast.194, s32[1024]{0:T(1024)S(1)} %pad_clamp_fusion), kind=kCustom, calls=%fused_computation | custom fusion | bytes 3145920 | tf_op jit(solution)/shard_map/jit(_take)/gather | solution.py:55
  108.3 1.9 fusion.36
  110.1 1.4 copy.66
  111.6 1.7 copy.65
  113.3 56.9 %while.10 = (s32[]{:T(128)}, bf16[12,4,32,1,64]{4,1,0,2,3:T(4,128)(2,1)}, s32[12,4,48]{2,1,0:T(4,128)}, bf16[12,4,32,1,64]{4,2,1,3,0:T(8,128)(2,1)}, bf16[48,128...) while((s32[]{:T(128)}, bf16[12,4,32,1,64]{4,1,0,2,3:T(4,128)(2,1)}, ...), condition=%wide.region_7.8_spmd, body=%wide.region_4.0_spmd.sunk | while | flops 210771904 | bytes 14258301 | solution.py:49
  114.0 1.5 fusion.56
  115.5 0.9 fusion.57
  116.5 1.0 fusion.58
  118.8 1.5 fusion.56
  121.2 1.0 fusion.58
  123.5 1.5 fusion.56
  125.9 1.0 fusion.58
  128.2 1.5 fusion.56
  130.7 1.0 fusion.58
  133.0 1.5 fusion.56
  135.4 1.0 fusion.58
  137.7 1.5 fusion.56
  140.1 1.0 fusion.58
  142.4 1.5 fusion.56
  144.9 1.0 fusion.58
  147.2 1.5 fusion.56
  149.6 1.0 fusion.58
  151.9 1.5 fusion.56
  154.4 1.0 fusion.58
  156.7 1.5 fusion.56
  159.1 1.0 fusion.58
  161.4 1.5 fusion.56
  163.9 1.0 fusion.58
  166.2 1.5 fusion.56
  168.6 1.0 fusion.58
  170.2 1.4 reshape.180
  171.6 18.1 %all_to_all.79 = bf16[8,2,6144]{2,1,0:T(2,128)(2,1)S(1)} all-to-all(bf16[8,2,6144]{2,1,0:T(2,128)(2,1)S(1)} %reshape.180), channel_id=1, replica_groups=mesh['rows'=64,'cols'=8] {'cols'}, dimensions={0} | all-to-all | bytes 393216 | tf_op jit(solution)/shard_map/all_to_all | solution.py:103
  (110 shorter events, 35.7 us)
Async XLA Ops:
  6.5 3.1 %copy-start = (bf16[512,1536]{1,0:T(8,128)(2,1)S(1)}, bf16[512,1536]{1,0:T(8,128)(2,1)}, u32[]{:S(2)}) copy-start(bf16[512,1536]{1,0:T(8,128)(2,1)} %param.14) | copy-start | bytes 4718596
  6.5 97.3 %all-gather.2.cloned.1.call-start = ((), (), s32[]{:S(2)}) async-start(), calls=%async_computation.5 | async-start | bytes 8519680 | tf_op jit(solution)/shard_map/all_gather | solution.py:54
  12.1 20.8 %all-to-all-start.1 = ((bf16[8,2,6144]{2,1,0:T(2,128)(2,1)}), bf16[8,2,6144]{2,1,0:T(2,128)(2,1)S(1)}, u32[]{:S(2)}, u32[]{:S(2)}) async-start(bf16[8,2,6144]{2,1,0:T(2,128)(2,1)} %reshape.174), calls=%async_computation.1 | async-start | bytes 393216 | tf_op jit(solution)/shard_map/all_to_all | solution.py:89
  32.9 16.4 %all-to-all-start = ((bf16[48,4,8,128]{3,1,0,2:T(4,128)(2,1)}), bf16[48,4,8,128]{3,1,0,2:T(4,128)(2,1)S(1)}, u32[]{:S(2)}, u32[]{:S(2)}) async-start(bf16[48,4,8,128]{3,1,0,2:T(4,128)(2,1)} %pad_maximum_fusion), calls=%async_computation | async-start | bytes 786432 | tf_op jit(solution)/shard_map/all_to_all | solution.py:90
  50.8 15.1 %copy-start.1 = (bf16[48,4,512]{2,1,0:T(4,128)(2,1)S(1)}, bf16[48,4,512]{2,1,0:T(4,128)(2,1)}, u32[]{:S(2)}) copy-start(bf16[48,4,512]{2,1,0:T(4,128)(2,1)} %param.12) | copy-start | bytes 589828
  50.8 15.1 %copy-start.3 = (bf16[512,512]{1,0:T(8,128)(2,1)S(1)}, bf16[512,512]{1,0:T(8,128)(2,1)}, u32[]{:S(2)}) copy-start(bf16[512,512]{1,0:T(8,128)(2,1)} %param.15) | copy-start | bytes 1572868
  52.4 13.9 %copy-start.5 = (f32[512]{0:T(512)S(1)}, f32[512]{0:T(512)}, u32[]{:S(2)}) copy-start(f32[512]{0:T(512)} %param.16) | copy-start | bytes 6148
  65.7 7.3 %copy-start.6 = (s32[1,48]{1,0:T(1,128)S(1)}, s32[1,48]{1,0:T(1,128)}, u32[]{:S(2)}) copy-start(s32[1,48]{1,0:T(1,128)} %param.20) | copy-start | bytes 580
  69.3 13.1 %all-to-all-start.3 = ((bf16[8,2,6144]{2,1,0:T(2,128)(2,1)}), bf16[8,2,6144]{2,1,0:T(2,128)(2,1)S(1)}, u32[]{:S(2)}, u32[]{:S(2)}) async-start(bf16[8,2,6144]{2,1,0:T(2,128)(2,1)} %reshape.178), calls=%async_computation.3 | async-start | bytes 393216 | tf_op jit(solution)/shard_map/all_to_all | solution.py:101
  114.0 2.4 %copy-start.2 = (bf16[48,128,1,64]{1,3,0,2:T(8,128)(2,1)S(1)}, bf16[48,128,1,64]{1,3,0,2:T(8,128)(2,1)}, u32[]{:S(2)}) copy-start(bf16[48,128,1,64]{1,3,0,2:T(8,128)(2,1)} %get-tuple-element.141) | copy-start | bytes 2359300 | tf_op jit(solution)/shard_map/while
  118.8 2.4 %copy-start.2 = (bf16[48,128,1,64]{1,3,0,2:T(8,128)(2,1)S(1)}, bf16[48,128,1,64]{1,3,0,2:T(8,128)(2,1)}, u32[]{:S(2)}) copy-start(bf16[48,128,1,64]{1,3,0,2:T(8,128)(2,1)} %get-tuple-element.141) | copy-start | bytes 2359300 | tf_op jit(solution)/shard_map/while
  123.5 2.4 %copy-start.2 = (bf16[48,128,1,64]{1,3,0,2:T(8,128)(2,1)S(1)}, bf16[48,128,1,64]{1,3,0,2:T(8,128)(2,1)}, u32[]{:S(2)}) copy-start(bf16[48,128,1,64]{1,3,0,2:T(8,128)(2,1)} %get-tuple-element.141) | copy-start | bytes 2359300 | tf_op jit(solution)/shard_map/while
  128.2 2.4 %copy-start.2 = (bf16[48,128,1,64]{1,3,0,2:T(8,128)(2,1)S(1)}, bf16[48,128,1,64]{1,3,0,2:T(8,128)(2,1)}, u32[]{:S(2)}) copy-start(bf16[48,128,1,64]{1,3,0,2:T(8,128)(2,1)} %get-tuple-element.141) | copy-start | bytes 2359300 | tf_op jit(solution)/shard_map/while
  133.0 2.4 %copy-start.2 = (bf16[48,128,1,64]{1,3,0,2:T(8,128)(2,1)S(1)}, bf16[48,128,1,64]{1,3,0,2:T(8,128)(2,1)}, u32[]{:S(2)}) copy-start(bf16[48,128,1,64]{1,3,0,2:T(8,128)(2,1)} %get-tuple-element.141) | copy-start | bytes 2359300 | tf_op jit(solution)/shard_map/while
  137.7 2.4 %copy-start.2 = (bf16[48,128,1,64]{1,3,0,2:T(8,128)(2,1)S(1)}, bf16[48,128,1,64]{1,3,0,2:T(8,128)(2,1)}, u32[]{:S(2)}) copy-start(bf16[48,128,1,64]{1,3,0,2:T(8,128)(2,1)} %get-tuple-element.141) | copy-start | bytes 2359300 | tf_op jit(solution)/shard_map/while
  142.4 2.4 %copy-start.2 = (bf16[48,128,1,64]{1,3,0,2:T(8,128)(2,1)S(1)}, bf16[48,128,1,64]{1,3,0,2:T(8,128)(2,1)}, u32[]{:S(2)}) copy-start(bf16[48,128,1,64]{1,3,0,2:T(8,128)(2,1)} %get-tuple-element.141) | copy-start | bytes 2359300 | tf_op jit(solution)/shard_map/while
  147.2 2.4 %copy-start.2 = (bf16[48,128,1,64]{1,3,0,2:T(8,128)(2,1)S(1)}, bf16[48,128,1,64]{1,3,0,2:T(8,128)(2,1)}, u32[]{:S(2)}) copy-start(bf16[48,128,1,64]{1,3,0,2:T(8,128)(2,1)} %get-tuple-element.141) | copy-start | bytes 2359300 | tf_op jit(solution)/shard_map/while
  151.9 2.4 %copy-start.2 = (bf16[48,128,1,64]{1,3,0,2:T(8,128)(2,1)S(1)}, bf16[48,128,1,64]{1,3,0,2:T(8,128)(2,1)}, u32[]{:S(2)}) copy-start(bf16[48,128,1,64]{1,3,0,2:T(8,128)(2,1)} %get-tuple-element.141) | copy-start | bytes 2359300 | tf_op jit(solution)/shard_map/while
  156.7 2.4 %copy-start.2 = (bf16[48,128,1,64]{1,3,0,2:T(8,128)(2,1)S(1)}, bf16[48,128,1,64]{1,3,0,2:T(8,128)(2,1)}, u32[]{:S(2)}) copy-start(bf16[48,128,1,64]{1,3,0,2:T(8,128)(2,1)} %get-tuple-element.141) | copy-start | bytes 2359300 | tf_op jit(solution)/shard_map/while
  161.4 2.4 %copy-start.2 = (bf16[48,128,1,64]{1,3,0,2:T(8,128)(2,1)S(1)}, bf16[48,128,1,64]{1,3,0,2:T(8,128)(2,1)}, u32[]{:S(2)}) copy-start(bf16[48,128,1,64]{1,3,0,2:T(8,128)(2,1)} %get-tuple-element.141) | copy-start | bytes 2359300 | tf_op jit(solution)/shard_map/while
  166.2 2.4 %copy-start.2 = (bf16[48,128,1,64]{1,3,0,2:T(8,128)(2,1)S(1)}, bf16[48,128,1,64]{1,3,0,2:T(8,128)(2,1)}, u32[]{:S(2)}) copy-start(bf16[48,128,1,64]{1,3,0,2:T(8,128)(2,1)} %get-tuple-element.141) | copy-start | bytes 2359300 | tf_op jit(solution)/shard_map/while
  170.2 20.3 %copy-start.4 = (bf16[512,512]{1,0:T(8,128)(2,1)S(1)}, bf16[512,512]{1,0:T(8,128)(2,1)}, u32[]{:S(2)}) copy-start(bf16[512,512]{1,0:T(8,128)(2,1)} %param.18) | copy-start | bytes 1572868
Sparse Core Ops, SparseCore 0:
  10.7 93.0 all-gather.1
where the time goes:
time: 200 us; the launch traced here: 198 us
  waiting for transfers between devices  51.3 us (26%)
  matrix products  34.6 us (17%)
  blocking collectives  30.2 us (15%)
  local copies, waits for them, and re-layouts  27.5 us (14%)
  other arithmetic  23.4 us (12%)
  starting transfers between devices  17.3 us (9%)
  between operations  13.8 us (7%)
    all_gather x1, waiting for transfers between devices, fetch_all(): gathered = lax.all_gather(tile_kv, 'rows', axis=0, tiled=True)  20 us
    all_to_all x1, blocking collectives, shards(): lax.all_to_all(answer, 'cols', split_axis=1, concat_axis=2, tiled=True)  18.1 us
    dot_general x12, matrix products, one_block(): jnp.einsum('rchd,tkhd->rchtk', block_q, key_part, preferred_element_type=...  17.6 us
    all_to_all x1, waiting for transfers between devices, shards(): lax.all_to_all(keyvals, 'cols', split_axis=2, concat_axis=1, tiled=True)  12.4 us
    all_to_all x1, blocking collectives, shards(): lax.all_to_all(mixed_col, 'cols', split_axis=1, concat_axis=2, tiled=True)  12.2 us
    dot_general x12, matrix products, one_block(): jnp.einsum('rchtk,tkhd->rchd', tile_weights, val_part, preferred_element_...  11.6 us
    reduce_sum x12, other arithmetic, soft_weights(): jnp.sum(expo_vals, axis=axes, keepdims=True)  11.4 us
    all_to_all x1, starting transfers between devices, shards(): lax.all_to_all(queries, 'cols', split_axis=2, concat_axis=1, tiled=True)  10.3 us
  transfers between devices with their start and end apart: 4, of which 4 were waited for; matrix products, arithmetic and copies ran while one was open for 8% of the time, Pallas kernels for 0%

commit v1 on v0

--- a/solution.py
+++ b/solution.py
@@ -51,7 +51,9 @@
 
 
 def fetch_all(tile_kv, tile_ids):
-    gathered = lax.all_gather(tile_kv, "rows", axis=0, tiled=True)
+    gathered = jnp.concatenate(
+        lax.all_to_all(jnp.stack([tile_kv] * lax.axis_size("rows")), "rows", 0, 0), axis=0
+    )
     return jnp.take(gathered, jnp.maximum(tile_ids[0], 0), axis=0)
 
 

time: 200 us -> 362 us (1.81)
  the two profiles are of different devices: /device:TPU:8 before, /device:TPU:10 now
where the time goes in v1:
time: 362 us; the launch traced here: 361 us
  waiting for transfers between devices  206 us (57%)
  blocking collectives  37.6 us (10%)
  matrix products  34.5 us (10%)
  local copies, waits for them, and re-layouts  33.6 us (9%)
  starting transfers between devices  24.6 us (7%)
  other arithmetic  23.5 us (6%)
    all_to_all x1, waiting for transfers between devices, fetch_all(): lax.all_to_all(jnp.stack([tile_kv] * lax.axis_size('rows')), 'rows', 0, 0)  185 us
    dot_general x12, matrix products, one_block(): jnp.einsum('rchd,tkhd->rchtk', block_q, key_part, preferred_element_type=...  17.6 us
    all_to_all x1, blocking collectives, shards(): lax.all_to_all(answer, 'cols', split_axis=1, concat_axis=2, tiled=True)  13.3 us
    all_to_all x1, waiting for transfers between devices, shards(): lax.all_to_all(keyvals, 'cols', split_axis=2, concat_axis=1, tiled=True)  12.4 us
    all_to_all x1, blocking collectives, shards(): lax.all_to_all(asked_q, 'cols', split_axis=2, concat_axis=1, tiled=True)  12.2 us
    all_to_all x1, blocking collectives, shards(): lax.all_to_all(mixed_col, 'cols', split_axis=1, concat_axis=2, tiled=True)  12.2 us
    dot_general x12, matrix products, one_block(): jnp.einsum('rchtk,tkhd->rchd', tile_weights, val_part, preferred_element_...  11.6 us
    reduce_sum x12, other arithmetic, soft_weights(): jnp.sum(expo_vals, axis=axes, keepdims=True)  11.4 us
  transfers between devices with their start and end apart: 3, of which 3 were waited for; matrix products, arithmetic and copies ran while one was open for 1% of the time, Pallas kernels for 0%

profile of v1, /device:TPU:10, one launch (start us, length us, event | category | flops | bytes accessed | tf_op | source)
XLA Modules:
  0.0 360.8 jit_solution(2429163687524007425)
XLA Ops:
  0.0 1.2 fusion.30
  1.2 1.1 fusion.32
  4.0 1.0 reshape.182
  5.0 10.3 %all-to-all-start.1 = ((bf16[8,2,6144]{2,1,0:T(2,128)(2,1)}), bf16[8,2,6144]{2,1,0:T(2,128)(2,1)S(1)}, u32[]{:S(2)}, u32[]{:S(2)}) async-start(bf16[8,2,6144]{2,1,0:T(2,128)(2,1)} %reshape.182), calls=%async_computation.1 | async-start | bytes 393216 | tf_op jit(solution)/shard_map/all_to_all | solution.py:91
  15.7 1.3 pad_maximum_fusion
  17.0 8.8 %all-to-all-done.1 = bf16[8,2,6144]{2,1,0:T(2,128)(2,1)S(1)} async-done(((bf16[8,2,6144]{2,1,0:T(2,128)(2,1)}), bf16[8,2,6144]{2,1,0:T(2,128)(2,1)S(1)}, u32[]{:S(2)}, u32[]{:S(2)}) %all-to-all-start.1) | async-done | bytes 196640 | tf_op jit(solution)/shard_map/all_to_all | solution.py:91
  25.8 3.5 all-to-all-start
  29.8 12.4 %all-to-all-done = bf16[48,4,8,128]{3,1,0,2:T(4,128)(2,1)S(1)} async-done(((bf16[48,4,8,128]{3,1,0,2:T(4,128)(2,1)}), bf16[48,4,8,128]{3,1,0,2:T(4,128)(2,1)S(1)}, u32[]{:S(2)}, u32[]{:S(2)}) %all-to-all-start) | async-done | bytes 393248 | tf_op jit(solution)/shard_map/all_to_all | solution.py:92
  42.4 1.3 fusion.38
  43.7 1.6 fusion.26
  45.8 12.2 %all_to_all.83 = bf16[8,2,6144]{2,1,0:T(2,128)(2,1)S(1)} all-to-all(bf16[8,2,6144]{2,1,0:T(2,128)(2,1)S(1)} %reshape.184), channel_id=1, replica_groups=mesh['rows'=64,'cols'=8] {'cols'}, dimensions={0} | all-to-all | bytes 393216 | tf_op jit(solution)/shard_map/all_to_all | solution.py:95
  59.5 1.3 convolution_convert_fusion.2
  61.5 12.2 %all_to_all.84 = bf16[8,2,6144]{2,1,0:T(2,128)(2,1)S(1)} all-to-all(bf16[8,2,6144]{2,1,0:T(2,128)(2,1)S(1)} %reshape.186), channel_id=1, replica_groups=mesh['rows'=64,'cols'=8] {'cols'}, dimensions={0} | all-to-all | bytes 393216 | tf_op jit(solution)/shard_map/all_to_all | solution.py:103
  73.7 5.3 %stack.2 = bf16[64,4,128,1,128]{4,2,1,3,0:T(8,128)(2,1)} broadcast(bf16[4,128,128]{2,1,0:T(8,128)(2,1)S(1)} %bitcast.194), dimensions={1,2,4} | broadcast | bytes 8519680 | tf_op jit(solution)/shard_map/stack | solution.py:55
  79.0 10.9 %all-to-all-start.4 = ((bf16[64,4,128,1,128]{4,2,1,3,0:T(8,128)(2,1)}), bf16[64,4,128,1,128]{4,2,1,3,0:T(8,128)(2,1)}, u32[]{:S(2)}, u32[]{:S(2)}) async-start(bf16[64,4,128,1,128]{4,2,1,3,0:T(8,128)(2,1)} %stack.2), calls=%async_computation.4 | async-start | bytes 16777216 | tf_op jit(solution)/shard_map/all_to_all | solution.py:55
  91.3 185.0 %all-to-all-done.4 = bf16[64,4,128,1,128]{4,2,1,3,0:T(8,128)(2,1)} async-done(((bf16[64,4,128,1,128]{4,2,1,3,0:T(8,128)(2,1)}), bf16[64,4,128,1,128]{4,2,1,3,0:T(8,128)(2,1)}, u32[]{:S(2)}, u32[]{:S(2)}) %all-to-all-start.4) | async-done | bytes 8388640 | tf_op jit(solution)/shard_map/all_to_all | solution.py:55
  276.3 4.2 %gather_fusion = bf16[48,128,128]{2,1,0:T(8,128)(2,1)S(1)} fusion(bf16[256,128,128]{2,1,0:T(8,128)(2,1)} %bitcast.41, s32[1024]{0:T(1024)S(1)} %pad_clamp_fusion), kind=kCustom, calls=%fused_computation | custom fusion | bytes 3145920 | tf_op jit(solution)/shard_map/jit(_take)/gather | solution.py:57
  280.8 2.3 fusion.36
  283.1 1.7 copy.64
  284.9 2.5 copy.65
  287.3 56.9 %while.10 = (s32[]{:T(128)}, bf16[12,4,32,1,64]{4,1,0,2,3:T(4,128)(2,1)}, s32[12,4,48]{2,1,0:T(4,128)}, bf16[12,4,32,1,64]{4,2,1,3,0:T(8,128)(2,1)}, bf16[48,128...) while((s32[]{:T(128)}, bf16[12,4,32,1,64]{4,1,0,2,3:T(4,128)(2,1)}, ...), condition=%wide.region_7.8_spmd, body=%wide.region_4.0_spmd.sunk | while | flops 210771904 | bytes 14259309 | solution.py:49
  288.0 1.5 fusion.56
  290.5 1.0 fusion.58
  292.8 1.5 fusion.56
  295.2 1.0 fusion.58
  297.5 1.5 fusion.56
  299.9 1.0 fusion.58
  302.2 1.5 fusion.56
  304.7 1.0 fusion.58
  307.0 1.5 fusion.56
  308.5 0.9 fusion.57
  309.4 1.0 fusion.58
  311.7 1.5 fusion.56
  314.2 1.0 fusion.58
  316.5 1.5 fusion.56
  318.9 1.0 fusion.58
  321.2 1.5 fusion.56
  323.7 1.0 fusion.58
  326.0 1.5 fusion.56
  328.4 1.0 fusion.58
  330.7 1.5 fusion.56
  333.1 1.0 fusion.58
  335.5 1.5 fusion.56
  337.9 1.0 fusion.58
  340.2 1.5 fusion.56
  342.6 1.0 fusion.58
  344.2 1.4 reshape.188
  345.6 13.3 %all_to_all.85 = bf16[8,2,6144]{2,1,0:T(2,128)(2,1)S(1)} all-to-all(bf16[8,2,6144]{2,1,0:T(2,128)(2,1)S(1)} %reshape.188), channel_id=1, replica_groups=mesh['rows'=64,'cols'=8] {'cols'}, dimensions={0} | all-to-all | bytes 393216 | tf_op jit(solution)/shard_map/all_to_all | solution.py:105
  (111 shorter events, 35.3 us)
Async XLA Ops:
  0.0 2.5 copy-start
  5.0 20.8 %all-to-all-start.1 = ((bf16[8,2,6144]{2,1,0:T(2,128)(2,1)}), bf16[8,2,6144]{2,1,0:T(2,128)(2,1)S(1)}, u32[]{:S(2)}, u32[]{:S(2)}) async-start(bf16[8,2,6144]{2,1,0:T(2,128)(2,1)} %reshape.182), calls=%async_computation.1 | async-start | bytes 393216 | tf_op jit(solution)/shard_map/all_to_all | solution.py:91
  25.8 16.4 %all-to-all-start = ((bf16[48,4,8,128]{3,1,0,2:T(4,128)(2,1)}), bf16[48,4,8,128]{3,1,0,2:T(4,128)(2,1)S(1)}, u32[]{:S(2)}, u32[]{:S(2)}) async-start(bf16[48,4,8,128]{3,1,0,2:T(4,128)(2,1)} %pad_maximum_fusion), calls=%async_computation | async-start | bytes 786432 | tf_op jit(solution)/shard_map/all_to_all | solution.py:92
  43.7 15.1 %copy-start.1 = (bf16[48,4,512]{2,1,0:T(4,128)(2,1)S(1)}, bf16[48,4,512]{2,1,0:T(4,128)(2,1)}, u32[]{:S(2)}) copy-start(bf16[48,4,512]{2,1,0:T(4,128)(2,1)} %param.12) | copy-start | bytes 589828
  43.7 15.1 %copy-start.3 = (bf16[512,512]{1,0:T(8,128)(2,1)S(1)}, bf16[512,512]{1,0:T(8,128)(2,1)}, u32[]{:S(2)}) copy-start(bf16[512,512]{1,0:T(8,128)(2,1)} %param.15) | copy-start | bytes 1572868
  45.3 13.9 %copy-start.6 = (f32[512]{0:T(512)S(1)}, f32[512]{0:T(512)}, u32[]{:S(2)}) copy-start(f32[512]{0:T(512)} %param.16) | copy-start | bytes 6148
  58.8 14.9 %copy-start.5 = (bf16[4,128,1,128]{3,1,2,0:T(8,128)(2,1)S(1)}, bf16[4,128,1,128]{3,1,2,0:T(8,128)(2,1)}, u32[]{:S(2)}) copy-start(bf16[4,128,1,128]{3,1,2,0:T(8,128)(2,1)} %param.19) | copy-start | bytes 393220
  79.0 10.9 %copy-start.7 = (s32[1,48]{1,0:T(1,128)S(1)}, s32[1,48]{1,0:T(1,128)}, u32[]{:S(2)}) copy-start(s32[1,48]{1,0:T(1,128)} %param.20) | copy-start | bytes 580
  79.0 197.3 %all-to-all-start.4 = ((bf16[64,4,128,1,128]{4,2,1,3,0:T(8,128)(2,1)}), bf16[64,4,128,1,128]{4,2,1,3,0:T(8,128)(2,1)}, u32[]{:S(2)}, u32[]{:S(2)}) async-start(bf16[64,4,128,1,128]{4,2,1,3,0:T(8,128)(2,1)} %stack.2), calls=%async_computation.4 | async-start | bytes 16777216 | tf_op jit(solution)/shard_map/all_to_all | solution.py:55
  288.0 2.4 copy-start.2
  292.8 2.4 copy-start.2
  297.5 2.4 copy-start.2
  302.2 2.4 copy-start.2
  307.0 2.4 copy-start.2
  311.7 2.4 copy-start.2
  316.5 2.4 copy-start.2
  321.2 2.4 copy-start.2
  326.0 2.4 copy-start.2
  330.7 2.4 copy-start.2
  335.5 2.4 copy-start.2
  340.2 2.4 copy-start.2
  344.2 15.5 %copy-start.4 = (bf16[512,512]{1,0:T(8,128)(2,1)S(1)}, bf16[512,512]{1,0:T(8,128)(2,1)}, u32[]{:S(2)}) copy-start(bf16[512,512]{1,0:T(8,128)(2,1)} %param.18) | copy-start | bytes 1572868
